TPU v7x, 32 devices: a whole 2x2x4 slice. The times are simulated.
32 devices in a mesh: dp: 8 (over z, x), mp: 4 (over y, core).
Axes of the slice: x: 2, y: 2, z: 4, core: 2. Of those that a mesh axis runs over, the one named last changes fastest.
Arguments:
- features: bfloat16 [8192, 1024], P('dp'), may hold values from -6 to 6
- out_grads: bfloat16 [8192, 4, 1024], P('dp', None, 'mp'), may hold values from -0.0625 to 0.0625
- norm_grads: float32 [8, 2048], P('dp'), may hold values from -2 to 2
- owners: int32 [5], replicated, may hold values from 0 to 7, as said below
- moment1: float32 [4, 1024, 1024], P(None, 'dp', 'mp'), may hold values from -6 to 6
- moment2: float32 [4, 1024, 1024], P(None, 'dp', 'mp'), may hold values from 0.1 to 10
- left_stats: float32 [4, 1024, 1024], P(None, 'dp', 'mp'), may hold values from -1024 to 1024, as said below
- right_stats: float32 [4, 1024, 1024], P(None, 'dp', 'mp'), may hold values from -1024 to 1024, as said below
- left_basis: float32 [4, 1024, 1024], P(None, 'dp', 'mp'), may hold values from -1 to 2
- right_basis: float32 [4, 1024, 1024], P(None, 'dp', 'mp'), may hold values from -1 to 2
- norm_m: float32 [2048], P('dp'), may hold values from -6 to 6
- norm_v: float32 [2048], P('dp'), may hold values from 0.1 to 10
Outputs:
- new_moment1: float32 [4, 1024, 1024], P(None, 'dp', 'mp')
- new_moment2: float32 [4, 1024, 1024], P(None, 'dp', 'mp')
- new_left_stats: float32 [4, 1024, 1024], P(None, 'dp', 'mp')
- new_right_stats: float32 [4, 1024, 1024], P(None, 'dp', 'mp')
- new_left_basis: float32 [4, 1024, 1024], P(None, 'dp', 'mp')
- new_right_basis: float32 [4, 1024, 1024], P(None, 'dp', 'mp')
- update_slots: bfloat16 [8, 1024, 1024], P('dp', None, 'mp')
- new_norm_m: float32 [2048], P('dp')
- new_norm_v: float32 [2048], P('dp')
- norm_slots: float32 [8, 2048], P('dp')
Inputs may be any that keep to these rules, and one draw needn't show every extreme that they name: `owners`: the first 4 entries are distinct, so a dp index owns at most one tile; the last entry may equal any of them. `left_stats`: each tile of statistics is symmetric. `right_stats`: each tile of statistics is symmetric.
All inputs are finite; a program needn't handle non-finite values.
Results may differ from a plain program's by a relative error of at most 0.0072.
Values may be sent and summed in bfloat16 or wider, within the bound.
A program may use at most 128 MiB of HBM per device.

v0:
```python
import jax
import jax.numpy as jnp
from jax import lax
from jax.sharding import PartitionSpec as P

FIX_ONE = 1.0 - 0.9**10
FIX_TWO = 1.0 - 0.95**10
BF = jnp.bfloat16
F32 = jnp.float32


def contract(left, right, left_dim, right_dim):
    return lax.dot_general(
        left, right, (((left_dim,), (right_dim,)), ((), ())), preferred_element_type=F32
    )


def to_tile(blocks):
    out = lax.all_to_all(blocks, "mp", split_axis=1, concat_axis=1, tiled=True)
    k, n, r, c = out.shape
    return out.transpose(0, 2, 1, 3).reshape(k, r, n * c)


def to_home(rows, n):
    k, r, c = rows.shape
    out = rows.reshape(k, r, n, c // n).transpose(0, 2, 1, 3)
    return lax.all_to_all(out, "mp", split_axis=1, concat_axis=1, tiled=True)


def gather_rows(rows):
    return lax.all_gather(rows, "dp", axis=0, tiled=True)


def normalize(power):
    wide = power.astype(F32)
    return lax.rsqrt(jnp.sum(wide * wide, axis=0, keepdims=True) + 1e-06)


def shards(
    features,
    out_grads,
    norm_grads,
    owners,
    moment1,
    moment2,
    left_stats,
    right_stats,
    left_basis,
    right_basis,
    norm_m,
    norm_v,
):
    dp = lax.axis_size("dp")
    tiles, slab, width = moment1.shape
    full = slab * dp
    me = lax.axis_index("dp")
    row0 = me * slab
    narrow = to_tile(jnp.stack([left_basis, right_basis, left_stats, right_stats]).astype(BF))
    left_full = gather_rows(narrow[0])
    right_full = gather_rows(narrow[1])
    flat = out_grads.reshape(out_grads.shape[0], tiles * width)
    partial = contract(features, flat, 0, 0).astype(BF).reshape(dp, slab, tiles * width)
    parts = lax.all_to_all(partial, "dp", split_axis=0, concat_axis=0, tiled=True)
    grad_home = jnp.sum(parts.astype(F32), axis=0).astype(BF)
    grad_home = grad_home.reshape(slab, tiles, width).transpose(1, 0, 2)
    grad_rows = to_tile(grad_home[None])[0]
    grad_full = gather_rows(grad_rows)
    wide = to_tile(jnp.stack([moment1, moment2]))
    prod_l = contract(grad_rows, grad_full, 1, 1)
    grad_cols = lax.dynamic_slice_in_dim(grad_full, row0, slab, 1)
    prod_r = contract(grad_cols, grad_full, 0, 0)
    stats_l = (0.95 * narrow[2].astype(F32) + 0.05 * prod_l).astype(BF)
    stats_r = (0.95 * narrow[3].astype(F32) + 0.05 * prod_r).astype(BF)
    power_l = contract(stats_l, left_full, 1, 0).astype(BF)
    power_r = contract(stats_r, right_full, 1, 0).astype(BF)
    power_l_full = gather_rows(power_l)
    power_r_full = gather_rows(power_r)
    left_cols = lax.dynamic_slice_in_dim(left_full, row0, slab, 1)
    half = contract(left_cols, grad_full, 0, 0).astype(BF)
    rotated = contract(half, right_full, 1, 0)
    tile_one = 0.9 * wide[0] + 0.1 * rotated
    tile_two = 0.95 * wide[1] + 0.05 * rotated * rotated
    direction = (tile_one / FIX_ONE / (jnp.sqrt(tile_two / FIX_TWO) + 1e-08)).astype(BF)
    back = contract(direction, right_full, 1, 1).astype(BF)
    back_full = gather_rows(back)
    home1 = to_home(jnp.stack([rotated, prod_l, prod_r]).astype(BF), tiles).astype(F32)
    new_one = 0.9 * moment1 + 0.1 * home1[0]
    new_two = 0.95 * moment2 + 0.05 * home1[0] * home1[0]
    new_sl = 0.95 * left_stats + 0.05 * home1[1]
    new_sr = 0.95 * right_stats + 0.05 * home1[2]
    update = contract(narrow[0], back_full, 1, 0).astype(BF)

    def refine(power_full, power_rows):
        scale = normalize(power_full)
        iter_full = (power_full.astype(F32) * scale).astype(BF)
        iter_rows = (power_rows.astype(F32) * scale).astype(BF)
        gram = contract(iter_rows, iter_full, 1, 1).astype(BF)
        return 1.5 * iter_rows.astype(F32) - 0.5 * contract(gram, iter_full, 1, 0)

    new_l = refine(power_l_full, power_l)
    new_r = refine(power_r_full, power_r)
    home2 = to_home(jnp.stack([new_l.astype(BF), new_r.astype(BF), update]), tiles)
    new_bl = home2[0].astype(F32)
    new_br = home2[1].astype(F32)
    slot_of = jnp.arange(dp, dtype=jnp.int32)[:, None, None]
    slots = jnp.zeros((dp, slab, width), BF)
    for n in range(tiles):
        slots = jnp.where(slot_of == owners[n], home2[2, n][None], slots)
    update_slot = lax.all_to_all(slots, "dp", split_axis=0, concat_axis=0, tiled=True)
    update_slot = update_slot.reshape(1, full, width)
    packed = jnp.concatenate([norm_grads[0], norm_m, norm_v])[None]
    everyone = lax.all_gather(packed, "dp", axis=0, tiled=True)
    size = norm_grads.shape[1]
    part = norm_m.shape[0]
    norm_total = jnp.sum(everyone[:, :size], axis=0)
    all_nm = 0.9 * everyone[:, size : size + part].reshape(size) + 0.1 * norm_total
    all_nv = 0.95 * everyone[:, size + part :].reshape(size) + 0.05 * norm_total * norm_total
    norm_step = all_nm / FIX_ONE / (jnp.sqrt(all_nv / FIX_TWO) + 1e-08)
    norm_slot = jnp.where(me == owners[tiles], norm_step, 0.0)[None]
    new_nm = lax.dynamic_slice_in_dim(all_nm, me * part, part, 0)
    new_nv = lax.dynamic_slice_in_dim(all_nv, me * part, part, 0)
    return (
        new_one,
        new_two,
        new_sl,
        new_sr,
        new_bl,
        new_br,
        update_slot,
        new_nm,
        new_nv,
        norm_slot,
    )


def solution(mesh):
    in_specs = (
        P("dp", None),
        P("dp", None, "mp"),
        P("dp", None),
        P(),
        P(None, "dp", "mp"),
        P(None, "dp", "mp"),
        P(None, "dp", "mp"),
        P(None, "dp", "mp"),
        P(None, "dp", "mp"),
        P(None, "dp", "mp"),
        P("dp"),
        P("dp"),
    )
    out_specs = (
        P(None, "dp", "mp"),
        P(None, "dp", "mp"),
        P(None, "dp", "mp"),
        P(None, "dp", "mp"),
        P(None, "dp", "mp"),
        P(None, "dp", "mp"),
        P("dp", None, "mp"),
        P("dp"),
        P("dp"),
        P("dp", None),
    )
    return jax.shard_map(shards, mesh=mesh, in_specs=in_specs, out_specs=out_specs, check_vma=False)
```

profile of v0, /device:TPU:0, one launch (start us, length us, event | category | flops | bytes accessed | tf_op | source)
XLA Modules:
  0.0 471.3 jit_solution(4801705262632254614)
XLA Ops:
  7.2 2.2 copy.123
  9.5 2.4 convolution_convert_fusion
  11.9 55.4 %all_to_all.35 = bf16[8,128,1024]{2,1,0:T(8,128)(2,1)} all-to-all(bf16[8,128,1024]{2,1,0:T(8,128)(2,1)S(1)} %bitcast.132), channel_id=1, replica_groups=mesh['dp'=8,'mp'=4] {'dp'}, dimensions={0} | all-to-all | bytes 4194304 | tf_op jit(solution)/shard_map/all_to_all | solution.py:63
  67.3 2.0 reduce_sum.41
  71.3 9.1 %all_to_all.36 = bf16[1,4,128,256]{3,2,0,1:T(8,128)(2,1)} all-to-all(bf16[1,4,128,256]{3,2,0,1:T(8,128)(2,1)S(1)} %copy.98), channel_id=1, replica_groups=mesh['dp'=8,'mp'=4] {'mp'}, dimensions={1} | all-to-all | bytes 524288 | tf_op jit(solution)/shard_map/all_to_all | solution.py:19
  85.2 16.9 %all_to_all.37 = bf16[4,4,128,256]{2,3,0,1:T(8,128)(2,1)S(1)} all-to-all(bf16[4,4,128,256]{2,3,0,1:T(8,128)(2,1)S(1)} %pad_maximum_fusion), channel_id=1, replica_groups=mesh['dp'=8,'mp'=4] {'mp'}, dimensions={1} | all-to-all | bytes 2097152 | tf_op jit(solution)/shard_map/all_to_all | solution.py:19
  106.1 24.6 %all-gather.11.cloned.1.call-done = bf16[1024,1024]{0,1:T(8,128)(2,1)} async-done(((bf16[128,1024]{0,1:T(8,128)(2,1)}), bf16[1024,1024]{0,1:T(8,128)(2,1)}) %all-gather.11.cloned.1.call-update) | async-done | bytes 2097168 | tf_op jit(solution)/shard_map/all_gather | solution.py:31
  130.6 3.4 fusion.89
  134.0 47.8 %all-gather.13.cloned.1.call-done = bf16[1024,1024]{0,1:T(8,128)(2,1)} async-done(((bf16[128,1024]{0,1:T(8,128)(2,1)}), bf16[1024,1024]{0,1:T(8,128)(2,1)}) %all-gather.13.cloned.1.call-update) | async-done | bytes 2097168 | tf_op jit(solution)/shard_map/all_gather | solution.py:31
  181.8 3.3 convolution_convert_fusion.3
  185.5 2.8 fusion.90
  188.2 44.8 %all-gather.9.cloned.1.call-done = bf16[1024,1024]{0,1:T(8,128)(2,1)} async-done(((bf16[128,1024]{0,1:T(8,128)(2,1)}), bf16[1024,1024]{0,1:T(8,128)(2,1)}) %all-gather.9.cloned.1.call-update) | async-done | bytes 2097168 | tf_op jit(solution)/shard_map/all_gather | solution.py:31
  233.0 3.1 convolution_convert_fusion.4
  238.8 17.0 %all_to_all.38 = f32[2,4,128,256]{2,3,0,1:T(8,128)S(1)} all-to-all(f32[2,4,128,256]{2,3,0,1:T(8,128)S(1)} %pad_maximum_fusion.1), channel_id=1, replica_groups=mesh['dp'=8,'mp'=4] {'mp'}, dimensions={1} | all-to-all | bytes 2097152 | tf_op jit(solution)/shard_map/all_to_all | solution.py:19
  257.2 4.8 %fusion.91 = (bf16[128,1024]{1,0:T(8,128)(2,1)}, f32[128,1024]{1,0:T(8,128)}) fusion(bf16[1024,1024]{0,1:T(8,128)(2,1)} %all-gather.13.cloned.1.call-done, bf16[1024,1024]{0,1:T(8,128)(2,1)} %all-gather.11.cloned.1.call-done, bf16[1024,1024]{0,1:T(8,128)(2,1)} %all-gather.9.cloned.1.call-done, s32[]{:T(128)S(6)} %select_n.36), kind=kOutput, calls=%fused_computation.119 | convolution fusion | flops 537133056 | bytes 5242884 | tf_op jit(solution)/shard_map/dot_general | solution.py:13
  261.9 3.1 convolution_convert_fusion.2
  265.8 17.1 %all-gather.17.cloned.1.call-done = bf16[1024,1024]{1,0:T(8,128)(2,1)} async-done(((bf16[128,1024]{1,0:T(8,128)(2,1)}), bf16[1024,1024]{1,0:T(8,128)(2,1)}) %all-gather.17.cloned.1.call-update) | async-done | bytes 2097168 | tf_op jit(solution)/shard_map/all_gather | solution.py:31
  282.9 2.1 fusion.2
  285.0 3.5 fusion.24
  288.7 43.9 %all-gather.15.cloned.1.call-done = bf16[1024,1024]{1,0:T(8,128)(2,1)} async-done(((bf16[128,1024]{1,0:T(8,128)(2,1)}), bf16[1024,1024]{1,0:T(8,128)(2,1)}) %all-gather.15.cloned.1.call-update) | async-done | bytes 2097168 | tf_op jit(solution)/shard_map/all_gather | solution.py:31
  332.5 2.1 fusion
  334.6 3.5 fusion.27
  338.4 44.4 %all-gather.19.cloned.1.call-done = bf16[1024,1024]{1,0:T(8,128)(2,1)} async-done(((bf16[128,1024]{1,0:T(8,128)(2,1)}), bf16[1024,1024]{1,0:T(8,128)(2,1)}) %all-gather.19.cloned.1.call-update) | async-done | bytes 2097168 | tf_op jit(solution)/shard_map/all_gather | solution.py:31
  382.7 2.1 convolution_convert_fusion.1
  386.0 3.6 all-to-all-start.5
  389.7 30.5 %all-gather.1 = f32[8,1,2560]{2,1,0:T(1,128)S(1)} all-gather(f32[1,1,2560]{2,1,0:T(1,128)S(1)} %reshape.191), channel_id=2, replica_groups=mesh['dp'=8,'mp'=4] {'dp'}, dimensions={0}, use_global_device_ids=true | all-gather | bytes 92160 | tf_op jit(solution)/shard_map/all_gather | solution.py:112
  421.6 1.8 stack.58
  427.9 2.0 maximum_bitcast_fusion
  429.9 4.2 all-to-all-start.3
  437.8 8.0 %all-to-all-done.3 = bf16[3,4,128,256]{3,2,0,1:T(8,128)(2,1)} async-done(((bf16[3,4,128,256]{3,2,0,1:T(8,128)(2,1)}), bf16[3,4,128,256]{3,2,0,1:T(8,128)(2,1)}, u32[]{:S(2)}, u32[]{:S(2)}) %all-to-all-start.3) | async-done | bytes 786464 | tf_op jit(solution)/shard_map/all_to_all | solution.py:27
  445.8 3.5 all-to-all-start.6
  453.8 9.8 %all-to-all-done.6 = bf16[8,128,256]{2,1,0:T(8,128)(2,1)S(1)} async-done(((bf16[8,128,256]{2,1,0:T(8,128)(2,1)}), bf16[8,128,256]{2,1,0:T(8,128)(2,1)S(1)}, u32[]{:S(2)}, u32[]{:S(2)}) %all-to-all-start.6) | async-done | bytes 524320 | tf_op jit(solution)/shard_map/all_to_all | solution.py:109
  (105 shorter events, 31.4 us)
Async XLA Ops:
  7.2 2.3 copy-start
  7.2 123.5 %all-gather.11.cloned.1.call-start = ((), (), s32[]{:S(2)}) async-start(), calls=%async_computation.8 | async-start | bytes 2359296 | tf_op jit(solution)/shard_map/all_gather | solution.py:31
  67.3 14.9 %copy-start.4 = (f32[4,128,256]{2,1,0:T(8,128)S(1)}, f32[4,128,256]{2,1,0:T(8,128)}, u32[]{:S(2)}) copy-start(f32[4,128,256]{2,1,0:T(8,128)} %param.19) | copy-start | bytes 1572868
  69.3 13.1 %copy-start.6 = (f32[4,128,256]{2,1,0:T(8,128)S(1)}, f32[4,128,256]{2,1,0:T(8,128)}, u32[]{:S(2)}) copy-start(f32[4,128,256]{2,1,0:T(8,128)} %param.18) | copy-start | bytes 1572868
  82.2 99.7 %all-gather.13.cloned.1.call-start = ((), (), s32[]{:S(2)}) async-start(), calls=%async_computation.9 | async-start | bytes 2359296 | tf_op jit(solution)/shard_map/all_gather | solution.py:31
  103.0 130.1 %all-gather.9.cloned.1.call-start = ((), (), s32[]{:S(2)}) async-start(), calls=%async_computation.7 | async-start | bytes 2359296 | tf_op jit(solution)/shard_map/all_gather | solution.py:31
  103.7 179.2 %all-gather.17.cloned.1.call-start = ((), (), s32[]{:S(2)}) async-start(), calls=%async_computation.11 | async-start | bytes 2359296 | tf_op jit(solution)/shard_map/all_gather | solution.py:31
  134.0 51.2 %copy-start.3 = (f32[1,128,4,256]{1,3,2,0:T(8,128)S(1)}, f32[1,128,4,256]{1,3,2,0:T(8,128)}, u32[]{:S(2)}) copy-start(f32[1,128,4,256]{1,3,2,0:T(8,128)} %get-tuple-element.14) | copy-start | bytes 1572868
  181.8 3.6 copy-start.1
  185.2 147.4 %all-gather.15.cloned.1.call-start = ((), (), s32[]{:S(2)}) async-start(), calls=%async_computation.10 | async-start | bytes 2359296 | tf_op jit(solution)/shard_map/all_gather | solution.py:31
  236.2 146.6 %all-gather.19.cloned.1.call-start = ((), (), s32[]{:S(2)}) async-start(), calls=%async_computation.12 | async-start | bytes 2359296 | tf_op jit(solution)/shard_map/all_gather | solution.py:31
  257.1 4.8 %copy-start.14 = (f32[128,1024]{1,0:T(8,128)S(1)}, f32[128,1024]{1,0:T(8,128)}, u32[]{:S(2)}) copy-start(f32[128,1024]{1,0:T(8,128)} %copy.118) | copy-start | bytes 1572868
  261.9 3.2 copy-start.16
  261.9 3.2 copy-start.17
  261.9 3.2 copy-start.18
  261.9 3.2 copy-start.15
  265.1 19.9 %copy-start.12 = (bf16[128,1024]{1,0:T(8,128)(2,1)S(1)}, bf16[128,1024]{1,0:T(8,128)(2,1)}, u32[]{:S(2)}) copy-start(bf16[128,1024]{1,0:T(8,128)(2,1)} %convolution_convert_fusion.3) | copy-start | bytes 786436
  288.4 46.2 %copy-start.13 = (bf16[128,1024]{1,0:T(8,128)(2,1)S(1)}, bf16[128,1024]{1,0:T(8,128)(2,1)}, u32[]{:S(2)}) copy-start(bf16[128,1024]{1,0:T(8,128)(2,1)} %convolution_convert_fusion.4) | copy-start | bytes 786436
  334.6 48.1 %copy-start.2 = (bf16[1,128,4,256]{1,3,2,0:T(8,128)(2,1)S(1)}, bf16[1,128,4,256]{1,3,2,0:T(8,128)(2,1)}, u32[]{:S(2)}) copy-start(bf16[1,128,4,256]{1,3,2,0:T(8,128)(2,1)} %get-tuple-element.18) | copy-start | bytes 786436
  385.0 40.0 %copy-start.10 = (bf16[128,1024]{1,0:T(8,128)(2,1)S(1)}, bf16[128,1024]{1,0:T(8,128)(2,1)}, u32[]{:S(2)}) copy-start(bf16[128,1024]{1,0:T(8,128)(2,1)} %get-tuple-element.37) | copy-start | bytes 786436
  386.0 41.6 %copy-start.11 = (bf16[128,1024]{1,0:T(8,128)(2,1)S(1)}, bf16[128,1024]{1,0:T(8,128)(2,1)}, u32[]{:S(2)}) copy-start(bf16[128,1024]{1,0:T(8,128)(2,1)} %get-tuple-element.39) | copy-start | bytes 786436
  386.0 43.9 %all-to-all-start.5 = ((bf16[3,4,128,256]{3,2,0,1:T(8,128)(2,1)}), bf16[3,4,128,256]{3,2,0,1:T(8,128)(2,1)S(1)}, u32[]{:S(2)}, u32[]{:S(2)}) async-start(bf16[3,4,128,256]{3,2,0,1:T(8,128)(2,1)} %maximum_bitcast_fusion.1), calls=%async_computation.5 | async-start | bytes 1572864 | tf_op jit(solution)/shard_map/all_to_all | solution.py:27
  429.9 15.9 %all-to-all-start.3 = ((bf16[3,4,128,256]{3,2,0,1:T(8,128)(2,1)}), bf16[3,4,128,256]{3,2,0,1:T(8,128)(2,1)}, u32[]{:S(2)}, u32[]{:S(2)}) async-start(bf16[3,4,128,256]{3,2,0,1:T(8,128)(2,1)} %maximum_bitcast_fusion), calls=%async_computation.3 | async-start | bytes 1572864 | tf_op jit(solution)/shard_map/all_to_all | solution.py:27
  445.8 17.9 %all-to-all-start.6 = ((bf16[8,128,256]{2,1,0:T(8,128)(2,1)}), bf16[8,128,256]{2,1,0:T(8,128)(2,1)S(1)}, u32[]{:S(2)}, u32[]{:S(2)}) async-start(bf16[8,128,256]{2,1,0:T(8,128)(2,1)} %select_select_fusion), calls=%async_computation.6 | async-start | bytes 1048576 | tf_op jit(solution)/shard_map/all_to_all | solution.py:109
  449.3 2.0 copy-start.5
  449.3 2.0 copy-start.7
  449.3 2.0 copy-start.8
  449.3 2.0 copy-start.9
Sparse Core Ops, SparseCore 0:
  82.3 48.3 all-gather.10
  133.3 48.5 all-gather.12
  184.5 48.5 all-gather.8
  235.6 47.2 all-gather.16
  284.9 47.6 all-gather.14
  335.1 47.6 all-gather.18
where the time goes:
time: 473 us; the launch traced here: 471 us
  waiting for transfers between devices  241 us (51%)
  blocking collectives  129 us (27%)
  matrix products  32 us (7%)
  local copies, waits for them, and re-layouts  23.3 us (5%)
  other arithmetic  19.3 us (4%)
  between operations  15.3 us (3%)
  starting transfers between devices  11.5 us (2%)
    all_gather x6, waiting for transfers between devices, gather_rows(): return lax.all_gather(rows, 'dp', axis=0, tiled=True)  222 us
    all_to_all x1, blocking collectives, shards(): lax.all_to_all(partial, 'dp', split_axis=0, concat_axis=0, tiled=True)  55.4 us
    all_to_all x3, blocking collectives, to_tile(): out = lax.all_to_all(blocks, 'mp', split_axis=1, concat_axis=1, tiled=True)  42.9 us
    dot_general x10, matrix products, contract(): lax.dot_general(left, right, (((left_dim,), (right_dim,)), ((), ())), pre...  32 us
    all_gather x1, blocking collectives, shards(): everyone = lax.all_gather(packed, 'dp', axis=0, tiled=True)  30.5 us
    all_to_all x1, waiting for transfers between devices, shards(): lax.all_to_all(slots, 'dp', split_axis=0, concat_axis=0, tiled=True)  9.82 us
  transfers between devices with their start and end apart: 9, of which 8 were waited for; matrix products, arithmetic and copies ran while one was open for 13% of the time, Pallas kernels for 0%

commit v1 on v0

--- a/solution.py
+++ b/solution.py
@@ -109,7 +109,10 @@
     update_slot = lax.all_to_all(slots, "dp", split_axis=0, concat_axis=0, tiled=True)
     update_slot = update_slot.reshape(1, full, width)
     packed = jnp.concatenate([norm_grads[0], norm_m, norm_v])[None]
-    everyone = lax.all_gather(packed, "dp", axis=0, tiled=True)
+    newest = lax.axis_size("dp")
+    carry = jnp.stack(newest * [packed])
+    response = lax.all_to_all(carry, "dp", split_axis=0, concat_axis=0)
+    everyone = jnp.concatenate(response, 0)
     size = norm_grads.shape[1]
     part = norm_m.shape[0]
     norm_total = jnp.sum(everyone[:, :size], axis=0)

time: 473 us -> 447 us (0.945)
  blocking collectives: 129 us -> 98.3 us
    all_gather x1 -> x0, blocking collectives: 30.5 us -> none  [shards(): everyone = lax.all_gather(packed, 'dp', axis=0, tiled=True)]
  transfers between devices with their start and end apart: 9 -> 10, of which waited for: 8 -> 8; matrix products, arithmetic and copies ran while one was open for 13% -> 14% of each run, Pallas kernels for 0% -> 0%
where the time goes in v1:
time: 447 us; the launch traced here: 445 us
  waiting for transfers between devices  241 us (54%)
  blocking collectives  98.3 us (22%)
  matrix products  32 us (7%)
  local copies, waits for them, and re-layouts  24.6 us (6%)
  other arithmetic  19.3 us (4%)
  between operations  15.3 us (3%)
  starting transfers between devices  15.1 us (3%)
    all_gather x6, waiting for transfers between devices, gather_rows(): return lax.all_gather(rows, 'dp', axis=0, tiled=True)  220 us
    all_to_all x1, blocking collectives, shards(): lax.all_to_all(partial, 'dp', split_axis=0, concat_axis=0, tiled=True)  55.4 us
    all_to_all x3, blocking collectives, to_tile(): out = lax.all_to_all(blocks, 'mp', split_axis=1, concat_axis=1, tiled=True)  42.9 us
    dot_general x10, matrix products, contract(): lax.dot_general(left, right, (((left_dim,), (right_dim,)), ((), ())), pre...  32 us
    all_to_all x2, waiting for transfers between devices, to_home(): return lax.all_to_all(out, 'mp', split_axis=1, concat_axis=1, tiled=True)  9.86 us
    all_to_all x1, waiting for transfers between devices, shards(): lax.all_to_all(slots, 'dp', split_axis=0, concat_axis=0, tiled=True)  9.82 us
    unnamed x55, local copies, waits for them, and re-layouts  9.04 us
  transfers between devices with their start and end apart: 10, of which 8 were waited for; matrix products, arithmetic and copies ran while one was open for 14% of the time, Pallas kernels for 0%

profile of v1, /device:TPU:0, one launch (start us, length us, event | category | flops | bytes accessed | tf_op | source)
XLA Modules:
  0.0 445.3 jit_solution(7328829045342619156)
XLA Ops:
  7.2 2.2 copy.123
  9.5 2.4 convolution_convert_fusion
  11.9 55.4 %all_to_all.40 = bf16[8,128,1024]{2,1,0:T(8,128)(2,1)} all-to-all(bf16[8,128,1024]{2,1,0:T(8,128)(2,1)S(1)} %bitcast.132), channel_id=1, replica_groups=mesh['dp'=8,'mp'=4] {'dp'}, dimensions={0} | all-to-all | bytes 4194304 | tf_op jit(solution)/shard_map/all_to_all | solution.py:63
  67.3 2.0 reduce_sum.41
  71.3 9.1 %all_to_all.41 = bf16[1,4,128,256]{3,2,0,1:T(8,128)(2,1)} all-to-all(bf16[1,4,128,256]{3,2,0,1:T(8,128)(2,1)S(1)} %copy.98), channel_id=1, replica_groups=mesh['dp'=8,'mp'=4] {'mp'}, dimensions={1} | all-to-all | bytes 524288 | tf_op jit(solution)/shard_map/all_to_all | solution.py:19
  85.2 16.9 %all_to_all.42 = bf16[4,4,128,256]{2,3,0,1:T(8,128)(2,1)S(1)} all-to-all(bf16[4,4,128,256]{2,3,0,1:T(8,128)(2,1)S(1)} %pad_maximum_fusion), channel_id=1, replica_groups=mesh['dp'=8,'mp'=4] {'mp'}, dimensions={1} | all-to-all | bytes 2097152 | tf_op jit(solution)/shard_map/all_to_all | solution.py:19
  106.1 24.6 %all-gather.9.cloned.1.call-done = bf16[1024,1024]{0,1:T(8,128)(2,1)} async-done(((bf16[128,1024]{0,1:T(8,128)(2,1)}), bf16[1024,1024]{0,1:T(8,128)(2,1)}) %all-gather.9.cloned.1.call-update) | async-done | bytes 2097168 | tf_op jit(solution)/shard_map/all_gather | solution.py:31
  130.7 3.4 fusion.89
  134.1 47.8 %all-gather.11.cloned.1.call-done = bf16[1024,1024]{0,1:T(8,128)(2,1)} async-done(((bf16[128,1024]{0,1:T(8,128)(2,1)}), bf16[1024,1024]{0,1:T(8,128)(2,1)}) %all-gather.11.cloned.1.call-update) | async-done | bytes 2097168 | tf_op jit(solution)/shard_map/all_gather | solution.py:31
  181.8 3.3 convolution_convert_fusion.3
  185.5 2.8 fusion.90
  188.2 44.8 %all-gather.7.cloned.1.call-done = bf16[1024,1024]{0,1:T(8,128)(2,1)} async-done(((bf16[128,1024]{0,1:T(8,128)(2,1)}), bf16[1024,1024]{0,1:T(8,128)(2,1)}) %all-gather.7.cloned.1.call-update) | async-done | bytes 2097168 | tf_op jit(solution)/shard_map/all_gather | solution.py:31
  233.0 3.1 convolution_convert_fusion.4
  238.8 17.0 %all_to_all.43 = f32[2,4,128,256]{2,3,0,1:T(8,128)S(1)} all-to-all(f32[2,4,128,256]{2,3,0,1:T(8,128)S(1)} %pad_maximum_fusion.1), channel_id=1, replica_groups=mesh['dp'=8,'mp'=4] {'mp'}, dimensions={1} | all-to-all | bytes 2097152 | tf_op jit(solution)/shard_map/all_to_all | solution.py:19
  257.1 4.8 %fusion.91 = (bf16[128,1024]{1,0:T(8,128)(2,1)}, f32[128,1024]{1,0:T(8,128)}) fusion(bf16[1024,1024]{0,1:T(8,128)(2,1)} %all-gather.11.cloned.1.call-done, bf16[1024,1024]{0,1:T(8,128)(2,1)} %all-gather.9.cloned.1.call-done, bf16[1024,1024]{0,1:T(8,128)(2,1)} %all-gather.7.cloned.1.call-done, s32[]{:T(128)S(6)} %select_n.36), kind=kOutput, calls=%fused_computation.119 | convolution fusion | flops 537133056 | bytes 5242884 | tf_op jit(solution)/shard_map/dot_general | solution.py:13
  261.9 3.1 convolution_convert_fusion.2
  265.8 3.5 all-to-all-start.7
  269.4 13.6 %all-gather.15.cloned.1.call-done = bf16[1024,1024]{1,0:T(8,128)(2,1)} async-done(((bf16[128,1024]{1,0:T(8,128)(2,1)}), bf16[1024,1024]{1,0:T(8,128)(2,1)}) %all-gather.15.cloned.1.call-update) | async-done | bytes 2097168 | tf_op jit(solution)/shard_map/all_gather | solution.py:31
  282.9 2.1 fusion.2
  285.0 48.4 %all-gather.13.cloned.1.call-done = bf16[1024,1024]{1,0:T(8,128)(2,1)} async-done(((bf16[128,1024]{1,0:T(8,128)(2,1)}), bf16[1024,1024]{1,0:T(8,128)(2,1)}) %all-gather.13.cloned.1.call-update) | async-done | bytes 2097168 | tf_op jit(solution)/shard_map/all_gather | solution.py:31
  333.4 2.1 fusion
  335.5 3.5 fusion.24
  339.0 3.5 fusion.27
  342.5 41.1 %all-gather.17.cloned.1.call-done = bf16[1024,1024]{1,0:T(8,128)(2,1)} async-done(((bf16[128,1024]{1,0:T(8,128)(2,1)}), bf16[1024,1024]{1,0:T(8,128)(2,1)}) %all-gather.17.cloned.1.call-update) | async-done | bytes 2097168 | tf_op jit(solution)/shard_map/all_gather | solution.py:31
  383.6 2.1 convolution_convert_fusion.1
  387.3 3.6 all-to-all-start.5
  395.5 1.8 stack.61
  401.8 2.0 maximum_bitcast_fusion
  403.8 4.2 all-to-all-start.3
  409.9 9.9 %all-to-all-done.3 = bf16[3,4,128,256]{3,2,0,1:T(8,128)(2,1)} async-done(((bf16[3,4,128,256]{3,2,0,1:T(8,128)(2,1)}), bf16[3,4,128,256]{3,2,0,1:T(8,128)(2,1)}, u32[]{:S(2)}, u32[]{:S(2)}) %all-to-all-start.3) | async-done | bytes 786464 | tf_op jit(solution)/shard_map/all_to_all | solution.py:27
  419.7 3.5 all-to-all-start.6
  427.8 9.8 %all-to-all-done.6 = bf16[8,128,256]{2,1,0:T(8,128)(2,1)S(1)} async-done(((bf16[8,128,256]{2,1,0:T(8,128)(2,1)}), bf16[8,128,256]{2,1,0:T(8,128)(2,1)S(1)}, u32[]{:S(2)}, u32[]{:S(2)}) %all-to-all-start.6) | async-done | bytes 524320 | tf_op jit(solution)/shard_map/all_to_all | solution.py:109
  (110 shorter events, 32.7 us)
Async XLA Ops:
  7.2 2.3 copy-start
  7.2 123.5 %all-gather.9.cloned.1.call-start = ((), (), s32[]{:S(2)}) async-start(), calls=%async_computation.9 | async-start | bytes 2359296 | tf_op jit(solution)/shard_map/all_gather | solution.py:31
  67.3 14.9 %copy-start.4 = (f32[4,128,256]{2,1,0:T(8,128)S(1)}, f32[4,128,256]{2,1,0:T(8,128)}, u32[]{:S(2)}) copy-start(f32[4,128,256]{2,1,0:T(8,128)} %param.19) | copy-start | bytes 1572868
  69.3 13.1 %copy-start.6 = (f32[4,128,256]{2,1,0:T(8,128)S(1)}, f32[4,128,256]{2,1,0:T(8,128)}, u32[]{:S(2)}) copy-start(f32[4,128,256]{2,1,0:T(8,128)} %param.18) | copy-start | bytes 1572868
  82.2 99.7 %all-gather.11.cloned.1.call-start = ((), (), s32[]{:S(2)}) async-start(), calls=%async_computation.10 | async-start | bytes 2359296 | tf_op jit(solution)/shard_map/all_gather | solution.py:31
  103.0 130.1 %all-gather.7.cloned.1.call-start = ((), (), s32[]{:S(2)}) async-start(), calls=%async_computation.8 | async-start | bytes 2359296 | tf_op jit(solution)/shard_map/all_gather | solution.py:31
  103.7 179.2 %all-gather.15.cloned.1.call-start = ((), (), s32[]{:S(2)}) async-start(), calls=%async_computation.12 | async-start | bytes 2359296 | tf_op jit(solution)/shard_map/all_gather | solution.py:31
  134.0 51.2 %copy-start.3 = (f32[1,128,4,256]{1,3,2,0:T(8,128)S(1)}, f32[1,128,4,256]{1,3,2,0:T(8,128)}, u32[]{:S(2)}) copy-start(f32[1,128,4,256]{1,3,2,0:T(8,128)} %get-tuple-element.14) | copy-start | bytes 1572868
  181.8 3.6 copy-start.1
  185.2 148.2 %all-gather.13.cloned.1.call-start = ((), (), s32[]{:S(2)}) async-start(), calls=%async_computation.11 | async-start | bytes 2359296 | tf_op jit(solution)/shard_map/all_gather | solution.py:31
  236.2 147.4 %all-gather.17.cloned.1.call-start = ((), (), s32[]{:S(2)}) async-start(), calls=%async_computation.13 | async-start | bytes 2359296 | tf_op jit(solution)/shard_map/all_gather | solution.py:31
  257.1 4.8 %copy-start.14 = (f32[128,1024]{1,0:T(8,128)S(1)}, f32[128,1024]{1,0:T(8,128)}, u32[]{:S(2)}) copy-start(f32[128,1024]{1,0:T(8,128)} %copy.118) | copy-start | bytes 1572868
  261.9 3.2 copy-start.18
  261.9 3.2 copy-start.19
  261.9 3.2 copy-start.20
  265.8 121.5 %all-to-all-start.7 = ((f32[8,1,2560]{2,1,0:T(1,128)}), f32[8,1,2560]{2,1,0:T(1,128)S(1)}, u32[]{:S(2)}, u32[]{:S(2)}) async-start(f32[8,1,2560]{2,1,0:T(1,128)} %stack.72), calls=%async_computation.7 | async-start | bytes 163840 | tf_op jit(solution)/shard_map/all_to_all | solution.py:114
  269.3 66.1 %copy-start.12 = (bf16[128,1024]{1,0:T(8,128)(2,1)S(1)}, bf16[128,1024]{1,0:T(8,128)(2,1)}, u32[]{:S(2)}) copy-start(bf16[128,1024]{1,0:T(8,128)(2,1)} %convolution_convert_fusion.3) | copy-start | bytes 786436
  335.5 3.5 copy-start.13
  339.0 44.6 %copy-start.2 = (bf16[1,128,4,256]{1,3,2,0:T(8,128)(2,1)S(1)}, bf16[1,128,4,256]{1,3,2,0:T(8,128)(2,1)}, u32[]{:S(2)}) copy-start(bf16[1,128,4,256]{1,3,2,0:T(8,128)(2,1)} %get-tuple-element.18) | copy-start | bytes 786436
  386.1 4.9 %copy-start.17 = (s32[5]{0:T(128)S(1)}, s32[5]{0:T(128)}, u32[]{:S(2)}) copy-start(s32[5]{0:T(128)} %param.15) | copy-start | bytes 64
  386.3 12.7 %copy-start.10 = (bf16[128,1024]{1,0:T(8,128)(2,1)S(1)}, bf16[128,1024]{1,0:T(8,128)(2,1)}, u32[]{:S(2)}) copy-start(bf16[128,1024]{1,0:T(8,128)(2,1)} %get-tuple-element.37) | copy-start | bytes 786436
  387.3 14.3 %copy-start.11 = (bf16[128,1024]{1,0:T(8,128)(2,1)S(1)}, bf16[128,1024]{1,0:T(8,128)(2,1)}, u32[]{:S(2)}) copy-start(bf16[128,1024]{1,0:T(8,128)(2,1)} %get-tuple-element.39) | copy-start | bytes 786436
  387.3 16.5 %all-to-all-start.5 = ((bf16[3,4,128,256]{3,2,0,1:T(8,128)(2,1)}), bf16[3,4,128,256]{3,2,0,1:T(8,128)(2,1)S(1)}, u32[]{:S(2)}, u32[]{:S(2)}) async-start(bf16[3,4,128,256]{3,2,0,1:T(8,128)(2,1)} %maximum_bitcast_fusion.1), calls=%async_computation.5 | async-start | bytes 1572864 | tf_op jit(solution)/shard_map/all_to_all | solution.py:27
  394.9 0.6 copy-start.15
  401.6 6.4 %copy-start.16 = (f32[8,1,2560]{2,0,1:T(8,128)S(1)}, f32[8,1,2560]{2,0,1:T(8,128)}, u32[]{:S(2)}) copy-start(f32[8,1,2560]{2,0,1:T(8,128)} %copy-done.15) | copy-start | bytes 245764
  403.8 15.9 %all-to-all-start.3 = ((bf16[3,4,128,256]{3,2,0,1:T(8,128)(2,1)}), bf16[3,4,128,256]{3,2,0,1:T(8,128)(2,1)}, u32[]{:S(2)}, u32[]{:S(2)}) async-start(bf16[3,4,128,256]{3,2,0,1:T(8,128)(2,1)} %maximum_bitcast_fusion), calls=%async_computation.3 | async-start | bytes 1572864 | tf_op jit(solution)/shard_map/all_to_all | solution.py:27
  419.7 17.9 %all-to-all-start.6 = ((bf16[8,128,256]{2,1,0:T(8,128)(2,1)}), bf16[8,128,256]{2,1,0:T(8,128)(2,1)S(1)}, u32[]{:S(2)}, u32[]{:S(2)}) async-start(bf16[8,128,256]{2,1,0:T(8,128)(2,1)} %select_select_fusion), calls=%async_computation.6 | async-start | bytes 1048576 | tf_op jit(solution)/shard_map/all_to_all | solution.py:109
  423.2 2.0 copy-start.5
  423.2 2.0 copy-start.7
  423.2 2.0 copy-start.8
  423.3 2.0 copy-start.9
Sparse Core Ops, SparseCore 0:
  82.3 48.3 all-gather.8
  133.3 48.5 all-gather.10
  184.5 48.5 all-gather.6
  235.6 47.2 all-gather.14
  284.9 48.4 all-gather.12
  335.9 47.6 all-gather.16
